TPU v7x, 32 devices: a whole 2x2x4 slice. The times are simulated.
32 devices in a mesh: groups: 2 (over x), tensor: 8 (over z, y), seq: 2 (over core).
Axes of the slice: x: 2, y: 2, z: 4, core: 2. Of those that a mesh axis runs over, the one named last changes fastest.
Arguments:
- heads_out: bfloat16 [128, 4096], P(('groups', 'seq'), 'tensor'), parts along dimension 0, may hold values from -6 to 6
- stream_in: bfloat16 [128, 8192], P(('groups', 'seq', 'tensor')), parts along dimension 0, may hold values from -40 to 40, as said below
- proj_levels: bfloat16 [4096, 8192], P('tensor'), may hold values from -8 to 7, as said below
- proj_scale: float32 [8192], replicated, may hold values from 0.001703125 to 0.006796875
- norm_gain: float32 [8192], replicated, may hold values from 0.25 to 1.75
- gate_levels: bfloat16 [8192, 14336], P(None, 'tensor'), may hold values from -8 to 7, as said below
- gate_scale: float32 [14336], P('tensor'), may hold values from 0.0012153398 to 0.004861359
- gate_index: int32 [8, 8], P('tensor'), may hold values from 0 to 1791, as said below
- gate_extra: bfloat16 [8192, 64], P(None, 'tensor'), may hold values from -0.29882812 to 0.29882812
- up_levels: bfloat16 [8192, 14336], P(None, 'tensor'), may hold values from -8 to 7, as said below
- up_scale: float32 [14336], P('tensor'), may hold values from 0.0012153398 to 0.004861359
- up_index: int32 [8, 8], P('tensor'), may hold values from 0 to 1791, as said below
- up_extra: bfloat16 [8192, 64], P(None, 'tensor'), may hold values from -0.29882812 to 0.29882812
- down_levels: bfloat16 [14336, 8192], P('tensor'), may hold values from -8 to 7, as said below
- down_scale: float32 [8192], replicated, may hold values from 0.0009020067 to 0.003591323
- down_index: int32 [8, 8], P('tensor'), may hold values from 0 to 8191, as said below
- down_extra: bfloat16 [14336, 8], P('tensor'), may hold values from -0.29882812 to 0.29882812
Outputs:
- stream_out: bfloat16 [128, 8192], P(('groups', 'seq', 'tensor')), parts along dimension 0
There are 2 independent parts, one for each index of `groups`. A program takes and returns all parts, laid end to end along the dimension named above; an argument that names none is the same for every part. Nothing has to cross between parts.
Inputs may be any that keep to these rules, and one draw needn't show every extreme that they name: stream_in has rows and columns of differing scales. `proj_levels`: integer values. `gate_levels`: integer values. `up_levels`: integer values. `down_levels`: integer values. `gate_index`: each row holds 8 different numbers. `up_index`: each row holds 8 different numbers. `down_index`: each row holds 8 different numbers.
All inputs are finite; a program needn't handle non-finite values.
Results may differ from a plain program's by a relative error of at most 0.0055.
Values may be sent and summed in bfloat16 or wider, within the bound.
No kernel may reach another device: no remote copies, remote signals or barrier semaphores. Data moves between devices by JAX's collectives and lax.ppermute only.
A program may use at most 192 MiB of HBM per device.

v0:
```python
import jax
import jax.numpy as jnp
from jax import lax
from jax.sharding import PartitionSpec as P


def rms_norm(mixed, norm_gain):
    mean_sq = jnp.mean(mixed * mixed, axis=-1, keepdims=True)
    return (mixed * lax.rsqrt(mean_sq + 1e-05) * norm_gain).astype(jnp.bfloat16)


def picker(index_row, width):
    return (index_row[:, None] == jnp.arange(width, dtype=jnp.int32)[None, :]).astype(jnp.float32)


def project(rows_in, levels, scale, extra, chosen):
    base = jnp.dot(rows_in, levels, preferred_element_type=jnp.float32)
    added = jnp.dot(rows_in, extra, preferred_element_type=jnp.float32)
    return base * scale + jnp.dot(added, chosen, precision=lax.Precision.HIGHEST)


def local(
    heads_out,
    stream_in,
    proj_levels,
    proj_scale,
    norm_gain,
    gate_levels,
    gate_scale,
    gate_index,
    gate_extra,
    up_levels,
    up_scale,
    up_index,
    up_extra,
    down_levels,
    down_scale,
    down_index,
    down_extra,
):
    own_rows = stream_in.shape[0]
    shard_width = gate_levels.shape[1]
    model_width = proj_levels.shape[1]
    gate_pick = picker(gate_index[0], shard_width)
    up_pick = picker(up_index[0], shard_width)
    down_pick = picker(down_index[0], model_width)
    total = lax.psum(
        jnp.dot(heads_out, proj_levels, preferred_element_type=jnp.float32) * proj_scale, "tensor"
    )
    stream_all = lax.all_gather(stream_in, "tensor", axis=0, tiled=True)
    mixed_all = stream_all.astype(jnp.float32) + total
    normed_rows = rms_norm(mixed_all, norm_gain)
    gate = project(normed_rows, gate_levels, gate_scale, gate_extra, gate_pick)
    up = project(normed_rows, up_levels, up_scale, up_extra, up_pick)
    hidden = (jax.nn.silu(gate) * up).astype(jnp.bfloat16)
    mixed = lax.dynamic_slice_in_dim(mixed_all, lax.axis_index("tensor") * own_rows, own_rows, 0)
    down = lax.psum_scatter(
        project(hidden, down_levels, down_scale, down_extra, down_pick),
        "tensor",
        scatter_dimension=0,
        tiled=True,
    )
    return (mixed + down).astype(jnp.bfloat16)


def solution(mesh):
    placed = (
        P(("groups", "seq"), "tensor"),
        P(("groups", "seq", "tensor"), None),
        P("tensor", None),
        P(),
        P(),
        P(None, "tensor"),
        P("tensor"),
        P("tensor", None),
        P(None, "tensor"),
        P(None, "tensor"),
        P("tensor"),
        P("tensor", None),
        P(None, "tensor"),
        P("tensor", None),
        P(),
        P("tensor", None),
        P("tensor", None),
    )
    return jax.shard_map(
        local,
        mesh=mesh,
        in_specs=placed,
        out_specs=P(("groups", "seq", "tensor"), None),
        check_vma=False,
    )
```

profile of v0, /device:TPU:0, one launch (start us, length us, event | category | flops | bytes accessed | tf_op | source)
XLA Modules:
  0.0 225.5 jit_solution(14587140887796130153)
XLA Ops:
  6.5 0.0 copy-start
  6.5 0.0 copy-start.4
  6.5 0.0 all-reduce.4.cloned.1.call-start
  6.5 6.0 %convolution_multiply_fusion.1 = f32[32,8192]{1,0:T(8,128)} fusion(bf16[32,512]{1,0:T(8,128)(2,1)} %param.17, bf16[512,8192]{1,0:T(8,128)(2,1)} %param.19, f32[8192]{0:T(1024)} %param.20), kind=kOutput, calls=%fused_computation.2 | convolution fusion | flops 268697600 | bytes 9502720 | tf_op jit(solution)/shard_map/dot_general | solution.py:48
  12.5 0.0 all-reduce.4.cloned.1.call-update
  12.6 0.0 all-reduce.6.cloned.1.call-start
  12.6 35.1 %all-gather = bf16[8,4,8192]{2,1,0:T(4,128)(2,1)S(1)} all-gather(bf16[1,4,8192]{2,1,0:T(4,128)(2,1)} %bitcast.22), channel_id=1, replica_groups=mesh['groups'=2,'tensor'=8,'seq'=2] {'tensor'}, dimensions={0}, use_global_device_ids=true | all-gather | bytes 589824 | tf_op jit(solution)/shard_map/all_gather | solution.py:50
  47.7 0.1 reshape.18
  47.8 48.7 %all-reduce.4.cloned.1.call-done = f32[32,8192]{1,0:T(8,128)} async-done(((f32[32,8192]{1,0:T(8,128)}), f32[32,8192]{1,0:T(8,128)}) %all-reduce.4.cloned.1.call-update) | async-done | bytes 1048592 | tf_op jit(solution)/shard_map/psum | solution.py:47
  96.4 1.4 multiply_reduce_fusion
  97.9 0.9 multiply_convert_fusion
  98.8 0.0 copy-done
  98.8 0.3 fusion.6
  99.1 1.2 fusion.7
  100.3 0.0 copy-start.5
  100.3 0.0 copy-start.7
  100.3 0.0 copy-start.3
  100.4 0.0 copy-start.2
  100.4 12.0 %convolution_multiply_fusion.3 = f32[32,1792]{1,0:T(8,128)S(1)} fusion(bf16[32,8192]{1,0:T(8,128)(2,1)S(1)} %multiply_convert_fusion, bf16[8192,1792]{1,0:T(8,128)(2,1)} %param.22, f32[1792]{0:T(1024)} %param.23), kind=kOutput, calls=%fused_computation.7 | convolution fusion | flops 939581440 | bytes 30120960 | tf_op jit(solution)/shard_map/dot_general | solution.py:17
  112.4 0.0 copy-done.4
  112.4 0.0 copy-start.6
  112.4 0.0 copy-start.8
  112.4 0.0 copy-start.1
  112.4 12.0 %convolution_multiply_fusion.2 = f32[32,1792]{1,0:T(8,128)S(1)} fusion(bf16[32,8192]{1,0:T(8,128)(2,1)S(1)} %multiply_convert_fusion, bf16[8192,1792]{1,0:T(8,128)(2,1)} %param.26, f32[1792]{0:T(1024)S(1)} %copy-done.4), kind=kOutput, calls=%fused_computation.5 | convolution fusion | flops 939581440 | bytes 30120960 | tf_op jit(solution)/shard_map/dot_general | solution.py:17
  124.4 0.0 copy-done.5
  124.4 0.3 convolution_add_fusion.2
  124.7 0.0 copy-done.7
  124.7 0.3 fusion.1
  125.0 0.0 copy-done.3
  125.1 0.1 fusion.8
  125.2 0.0 copy-done.2
  125.2 12.0 %convolution_multiply_fusion = f32[32,8192]{1,0:T(8,128)S(1)} fusion(bf16[32,1792]{1,0:T(8,128)(2,1)S(1)} %fusion.1, bf16[1792,8192]{1,0:T(8,128)(2,1)} %param.30, f32[8192]{0:T(1024)S(1)} %copy-done.2), kind=kOutput, calls=%fused_computation.1 | convolution fusion | flops 939786240 | bytes 30556160 | tf_op jit(solution)/shard_map/dot_general | solution.py:17
  137.2 0.0 copy-done.6
  137.2 1.7 convolution_add_fusion
  138.9 0.0 all-reduce.6.cloned.1.call-update
  138.9 0.0 copy-done.8
  139.0 0.6 dynamic-slice
  140.2 76.8 %all-reduce.6.cloned.1.call-done = f32[32,8192]{1,0:T(8,128)} async-done(((f32[32,8192]{1,0:T(8,128)}), f32[32,8192]{1,0:T(8,128)}) %all-reduce.6.cloned.1.call-update) | async-done | bytes 1048592
  217.0 1.6 fusion.2
  218.7 0.0 copy-done.1
  (1 shorter events, 0.0 us)
Async XLA Ops:
  6.5 92.3 %copy-start = (bf16[8192,8]{0,1:T(8,128)(2,1)S(1)}, bf16[8192,8]{0,1:T(8,128)(2,1)}, u32[]{:S(2)}) copy-start(bf16[8192,8]{0,1:T(8,128)(2,1)} %param.25) | copy-start | bytes 393220
  6.5 105.8 %copy-start.4 = (f32[1792]{0:T(1024)S(1)}, f32[1792]{0:T(1024)}, u32[]{:S(2)}) copy-start(f32[1792]{0:T(1024)} %param.27) | copy-start | bytes 21508
  6.5 89.9 %all-reduce.4.cloned.1.call-start = ((), (), s32[]{:S(2)}) async-start(), calls=%async_computation | async-start | bytes 2097152 | tf_op jit(solution)/shard_map/psum | solution.py:47
  12.6 204.5 %all-reduce.6.cloned.1.call-start = ((), (), s32[]{:S(2)}) async-start(), calls=%async_computation.1 | async-start | bytes 2097152
  100.3 24.1 %copy-start.5 = (s32[1,8]{1,0:T(1,128)S(1)}, s32[1,8]{1,0:T(1,128)}, u32[]{:S(2)}) copy-start(s32[1,8]{1,0:T(1,128)} %param.24) | copy-start | bytes 100
  100.3 24.4 %copy-start.7 = (s32[1,8]{1,0:T(1,128)S(1)}, s32[1,8]{1,0:T(1,128)}, u32[]{:S(2)}) copy-start(s32[1,8]{1,0:T(1,128)} %param.28) | copy-start | bytes 100
  100.3 24.7 %copy-start.3 = (bf16[1792,8]{0,1:T(8,128)(2,1)S(1)}, bf16[1792,8]{0,1:T(8,128)(2,1)}, u32[]{:S(2)}) copy-start(bf16[1792,8]{0,1:T(8,128)(2,1)} %param.33) | copy-start | bytes 86020
  100.4 24.8 %copy-start.2 = (f32[8192]{0:T(1024)S(1)}, f32[8192]{0:T(1024)}, u32[]{:S(2)}) copy-start(f32[8192]{0:T(1024)} %param.31) | copy-start | bytes 98308
  112.4 24.9 %copy-start.6 = (s32[1,8]{1,0:T(1,128)S(1)}, s32[1,8]{1,0:T(1,128)}, u32[]{:S(2)}) copy-start(s32[1,8]{1,0:T(1,128)} %param.32) | copy-start | bytes 100
  112.4 26.6 %copy-start.8 = (u32[32]{0:T(128)S(1)}, u32[32]{0:T(128)}, u32[]{:S(2)}) copy-start(u32[32]{0:T(128)} %constant.28) | copy-start | bytes 388
  112.4 106.3 %copy-start.1 = (bf16[8192,8]{0,1:T(8,128)(2,1)S(1)}, bf16[8192,8]{0,1:T(8,128)(2,1)}, u32[]{:S(2)}) copy-start(bf16[8192,8]{0,1:T(8,128)(2,1)} %param.25) | copy-start | bytes 393220
Sparse Core Ops, SparseCore 0:
  12.7 83.7 all-reduce.3
  139.1 77.9 all-reduce.5
where the time goes:
time: 226 us
  waiting for transfers between devices  126 us (56%)
  matrix products  45.9 us (20%)
  blocking collectives  35.1 us (16%)
  between operations  14.2 us (6%)
  other arithmetic  4.02 us (2%)
    unnamed x3, waiting for transfers between devices  76.9 us
    psum x1, waiting for transfers between devices, local(): lax.psum(jnp.dot(heads_out, proj_levels, preferred_element_type=jnp.float...  48.7 us
    dot_general x3, matrix products, project(): base = jnp.dot(rows_in, levels, preferred_element_type=jnp.float32)  36 us
    all_gather x1, blocking collectives, local(): stream_all = lax.all_gather(stream_in, 'tensor', axis=0, tiled=True)  35.1 us
    dot_general x1, matrix products, local(): jnp.dot(heads_out, proj_levels, preferred_element_type=jnp.float32)  6 us
  transfers between devices with their start and end apart: 2, of which 2 were waited for; matrix products, arithmetic and copies ran while one was open for 0% of the time, Pallas kernels for 0%

commit v1 on v0

--- a/solution.py
+++ b/solution.py
@@ -44,8 +44,12 @@
     gate_pick = picker(gate_index[0], shard_width)
     up_pick = picker(up_index[0], shard_width)
     down_pick = picker(down_index[0], model_width)
-    total = lax.psum(
-        jnp.dot(heads_out, proj_levels, preferred_element_type=jnp.float32) * proj_scale, "tensor"
+    total = jnp.sum(
+        lax.all_gather(
+            jnp.dot(heads_out, proj_levels, preferred_element_type=jnp.float32) * proj_scale,
+            "tensor",
+        ),
+        axis=0,
     )
     stream_all = lax.all_gather(stream_in, "tensor", axis=0, tiled=True)
     mixed_all = stream_all.astype(jnp.float32) + total

time: 226 us -> 272 us (1.20)
  waiting for transfers between devices: 126 us -> 170 us
    all_gather x0 -> x1, waiting for transfers between devices: none -> 94.7 us  [local(): lax.all_gather(jnp.dot(heads_out, proj_levels, preferred_element_type=jnp...]
    psum x1 -> x0, waiting for transfers between devices: 48.7 us -> none  [local(): lax.psum(jnp.dot(heads_out, proj_levels, preferred_element_type=jnp.float...]
    reduce_sum x0 -> x1, other arithmetic: none -> 3.91 us  [local(): jnp.sum(lax.all_gather(jnp.dot(heads_out, proj_levels, preferred_element_...]
where the time goes in v1:
time: 272 us
  waiting for transfers between devices  170 us (62%)
  matrix products  45 us (17%)
  blocking collectives  35.5 us (13%)
  between operations  14.3 us (5%)
  other arithmetic  5.94 us (2%)
    all_gather x1, waiting for transfers between devices, local(): lax.all_gather(jnp.dot(heads_out, proj_levels, preferred_element_type=jnp...  94.7 us
    unnamed x3, waiting for transfers between devices  75.4 us
    dot_general x3, matrix products, project(): base = jnp.dot(rows_in, levels, preferred_element_type=jnp.float32)  36 us
    all_gather x1, blocking collectives, local(): stream_all = lax.all_gather(stream_in, 'tensor', axis=0, tiled=True)  35.5 us
    dot_general x1, matrix products, local(): jnp.dot(heads_out, proj_levels, preferred_element_type=jnp.float32)  6.07 us
  transfers between devices with their start and end apart: 2, of which 2 were waited for; matrix products, arithmetic and copies ran while one was open for 0% of the time, Pallas kernels for 0%

profile of v1, /device:TPU:0, one launch (start us, length us, event | category | flops | bytes accessed | tf_op | source)
XLA Modules:
  0.0 271.6 jit_solution(10732890700718917495)
XLA Ops:
  6.5 0.0 copy-start
  6.5 0.0 copy-start.3
  6.5 0.0 copy-start.9
  6.5 0.0 copy-start.5
  6.5 0.0 all-gather.4.cloned.1.call-start
  6.6 6.1 %convolution_multiply_fusion.1 = f32[32,8192]{1,0:T(8,128)} fusion(bf16[32,512]{1,0:T(8,128)(2,1)} %param.17, bf16[512,8192]{1,0:T(8,128)(2,1)} %param.19, f32[8192]{0:T(1024)} %param.20), kind=kOutput, calls=%fused_computation.2 | convolution fusion | flops 268697600 | bytes 9502720 | tf_op jit(solution)/shard_map/dot_general | solution.py:49
  12.7 0.0 copy-start.6
  12.7 0.0 all-gather.4.cloned.1.call-update
  12.7 0.0 all-reduce.3.cloned.1.call-start
  12.7 35.5 %all-gather.1 = bf16[8,4,8192]{2,1,0:T(4,128)(2,1)S(1)} all-gather(bf16[1,4,8192]{2,1,0:T(4,128)(2,1)} %bitcast.24), channel_id=1, replica_groups=mesh['groups'=2,'tensor'=8,'seq'=2] {'tensor'}, dimensions={0}, use_global_device_ids=true | all-gather | bytes 589824 | tf_op jit(solution)/shard_map/all_gather | solution.py:54
  48.2 0.1 reshape.19
  48.3 94.7 %all-gather.4.cloned.1.call-done = f32[256,8192]{1,0:T(8,128)} async-done(((f32[32,8192]{1,0:T(8,128)}), f32[256,8192]{1,0:T(8,128)}) %all-gather.4.cloned.1.call-update) | async-done | bytes 8388624 | tf_op jit(solution)/shard_map/all_gather | solution.py:48
  143.1 3.9 %reduce_sum.18 = f32[32,8192]{1,0:T(8,128)S(1)} reduce(f32[8,32,8192]{2,1,0:T(8,128)} %bitcast.23, f32[]{:T(128)} %constant.4.clone.1), dimensions={0}, to_apply=%region_0.0 | reduce | flops 1835008 | bytes 9437188 | tf_op jit(solution)/shard_map/reduce_sum | solution.py:47
  147.0 0.2 multiply_reduce_fusion
  147.2 0.0 copy-done.3
  147.2 0.2 multiply_convert_fusion
  147.4 0.0 copy-done
  147.4 0.3 fusion.6
  147.7 0.0 copy-done.9
  147.7 0.3 fusion.7
  148.0 0.0 copy-done.5
  148.0 0.0 copy-start.7
  148.0 0.0 copy-start.10
  148.0 0.0 copy-start.4
  148.0 0.0 copy-start.2
  148.0 12.0 %convolution_multiply_fusion.3 = f32[32,1792]{1,0:T(8,128)S(1)} fusion(bf16[32,8192]{1,0:T(8,128)(2,1)S(1)} %multiply_convert_fusion, bf16[8192,1792]{1,0:T(8,128)(2,1)} %param.22, f32[1792]{0:T(1024)S(1)} %copy-done.5), kind=kOutput, calls=%fused_computation.7 | convolution fusion | flops 939581440 | bytes 30120960 | tf_op jit(solution)/shard_map/dot_general | solution.py:17
  160.0 0.0 copy-done.6
  160.0 0.0 copy-start.8
  160.0 0.0 copy-start.11
  160.0 0.0 copy-start.1
  160.0 12.0 %convolution_multiply_fusion.2 = f32[32,1792]{1,0:T(8,128)S(1)} fusion(bf16[32,8192]{1,0:T(8,128)(2,1)S(1)} %multiply_convert_fusion, bf16[8192,1792]{1,0:T(8,128)(2,1)} %param.26, f32[1792]{0:T(1024)S(1)} %copy-done.6), kind=kOutput, calls=%fused_computation.5 | convolution fusion | flops 939581440 | bytes 30120960 | tf_op jit(solution)/shard_map/dot_general | solution.py:17
  172.0 0.0 copy-done.7
  172.1 0.3 convolution_add_fusion.2
  172.4 0.0 copy-done.10
  172.4 0.3 fusion.1
  172.7 0.0 copy-done.4
  172.7 0.1 fusion.8
  172.8 0.0 copy-done.2
  172.8 12.0 %convolution_multiply_fusion = f32[32,8192]{1,0:T(8,128)S(1)} fusion(bf16[32,1792]{1,0:T(8,128)(2,1)S(1)} %fusion.1, bf16[1792,8192]{1,0:T(8,128)(2,1)} %param.30, f32[8192]{0:T(1024)S(1)} %copy-done.2), kind=kOutput, calls=%fused_computation.1 | convolution fusion | flops 939786240 | bytes 30556160 | tf_op jit(solution)/shard_map/dot_general | solution.py:17
  184.9 0.0 copy-done.8
  184.9 1.6 convolution_add_fusion
  186.5 0.0 all-reduce.3.cloned.1.call-update
  186.6 0.0 copy-done.11
  186.6 0.6 dynamic-slice
  187.8 75.3 %all-reduce.3.cloned.1.call-done = f32[32,8192]{1,0:T(8,128)} async-done(((f32[32,8192]{1,0:T(8,128)}), f32[32,8192]{1,0:T(8,128)}) %all-reduce.3.cloned.1.call-update) | async-done | bytes 1048592
  263.2 1.6 fusion.2
  264.8 0.0 copy-done.1
  (1 shorter events, 0.0 us)
Async XLA Ops:
  6.5 140.8 %copy-start = (bf16[8192,8]{0,1:T(8,128)(2,1)S(1)}, bf16[8192,8]{0,1:T(8,128)(2,1)}, u32[]{:S(2)}) copy-start(bf16[8192,8]{0,1:T(8,128)(2,1)} %param.25) | copy-start | bytes 393220
  6.5 140.7 %copy-start.3 = (f32[8192]{0:T(1024)S(1)}, f32[8192]{0:T(1024)}, u32[]{:S(2)}) copy-start(f32[8192]{0:T(1024)} %param.21) | copy-start | bytes 98308
  6.5 141.1 %copy-start.9 = (bf16[8192,8]{0,1:T(8,128)(2,1)S(1)}, bf16[8192,8]{0,1:T(8,128)(2,1)}, u32[]{:S(2)}) copy-start(bf16[8192,8]{0,1:T(8,128)(2,1)} %param.29) | copy-start | bytes 393220
  6.5 141.4 %copy-start.5 = (f32[1792]{0:T(1024)S(1)}, f32[1792]{0:T(1024)}, u32[]{:S(2)}) copy-start(f32[1792]{0:T(1024)} %param.23) | copy-start | bytes 21508
  6.5 136.5 %all-gather.4.cloned.1.call-start = ((), (), s32[]{:S(2)}) async-start(), calls=%async_computation | async-start | bytes 9437184 | tf_op jit(solution)/shard_map/all_gather | solution.py:48
  12.7 147.3 %copy-start.6 = (f32[1792]{0:T(1024)S(1)}, f32[1792]{0:T(1024)}, u32[]{:S(2)}) copy-start(f32[1792]{0:T(1024)} %param.27) | copy-start | bytes 21508
  12.7 250.5 %all-reduce.3.cloned.1.call-start = ((), (), s32[]{:S(2)}) async-start(), calls=%async_computation.1 | async-start | bytes 2097152
  148.0 24.1 %copy-start.7 = (s32[1,8]{1,0:T(1,128)S(1)}, s32[1,8]{1,0:T(1,128)}, u32[]{:S(2)}) copy-start(s32[1,8]{1,0:T(1,128)} %param.24) | copy-start | bytes 100
  148.0 24.4 %copy-start.10 = (s32[1,8]{1,0:T(1,128)S(1)}, s32[1,8]{1,0:T(1,128)}, u32[]{:S(2)}) copy-start(s32[1,8]{1,0:T(1,128)} %param.28) | copy-start | bytes 100
  148.0 24.7 %copy-start.4 = (bf16[1792,8]{0,1:T(8,128)(2,1)S(1)}, bf16[1792,8]{0,1:T(8,128)(2,1)}, u32[]{:S(2)}) copy-start(bf16[1792,8]{0,1:T(8,128)(2,1)} %param.33) | copy-start | bytes 86020
  148.0 24.8 %copy-start.2 = (f32[8192]{0:T(1024)S(1)}, f32[8192]{0:T(1024)}, u32[]{:S(2)}) copy-start(f32[8192]{0:T(1024)} %param.31) | copy-start | bytes 98308
  160.0 24.9 %copy-start.8 = (s32[1,8]{1,0:T(1,128)S(1)}, s32[1,8]{1,0:T(1,128)}, u32[]{:S(2)}) copy-start(s32[1,8]{1,0:T(1,128)} %param.32) | copy-start | bytes 100
  160.0 26.5 %copy-start.11 = (u32[32]{0:T(128)S(1)}, u32[32]{0:T(128)}, u32[]{:S(2)}) copy-start(u32[32]{0:T(128)} %constant.28) | copy-start | bytes 388
  160.0 104.8 %copy-start.1 = (bf16[8192,8]{0,1:T(8,128)(2,1)S(1)}, bf16[8192,8]{0,1:T(8,128)(2,1)}, u32[]{:S(2)}) copy-start(bf16[8192,8]{0,1:T(8,128)(2,1)} %param.25) | copy-start | bytes 393220
Sparse Core Ops, SparseCore 0:
  12.8 130.2 all-gather.3
  186.7 76.4 all-reduce.2
